TPU v7x, 32 devices: a whole 2x2x4 slice. The times are simulated.
32 devices in a mesh: row: 8 (over y, x, core), col: 4 (over z).
Axes of the slice: x: 2, y: 2, z: 4, core: 2. Of those that a mesh axis runs over, the one named last changes fastest.
Arguments:
- rhs: float32 [32, 1024, 4096], P(None, 'row', 'col'), may hold values from -6 to 6
- factor: bfloat16 [32, 1024, 4, 1024], P(None, 'row', None, 'col'), may hold values from -0.09375 to 0.09375
- diag_inverse: bfloat16 [4, 1024, 1024], P(None, 'row'), may hold values from -1.5 to 1.5, as said below
Outputs:
- solution: float32 [4, 1024, 4096], P(None, 'row', 'col')
- remaining: float32 [28, 1024, 4096], P(None, 'row', 'col')
Inputs may be any that keep to these rules, and one draw needn't show every extreme that they name: Each diag_inverse[k] is lower triangular with diagonal entries from 0.5 to 1.5.
All inputs are finite; a program needn't handle non-finite values.
Results may differ from a plain program's by a relative error of at most 0.0044.
Values may be sent and summed in bfloat16 or wider, within the bound.
A program may use at most 192 MiB of HBM per device.

v0:
```python
import jax
import jax.numpy as jnp
from jax import lax
from jax.sharding import PartitionSpec as P

STEPS = 4


def shards(rhs, factor, diag_inverse):
    block_count, tile_rows, rhs_width = rhs.shape
    panel_cols = factor.shape[3]
    remaining_rows = rhs
    solved_list = []
    for section in range(STEPS):
        current = remaining_rows[0].astype(jnp.bfloat16)
        inverse_section = diag_inverse[section]
        own_rows = jnp.dot(
            inverse_section,
            lax.all_gather(current, "row", axis=0, tiled=True),
            preferred_element_type=jnp.float32,
        )
        whole_solved = lax.all_gather(own_rows.astype(jnp.bfloat16), "row", axis=0, tiled=True)
        solved_list.append(own_rows)
        later_count = block_count - section - 1
        lower_tiles = factor[section + 1 :, :, section, :]
        flat_tiles = lower_tiles.reshape(later_count * tile_rows, panel_cols)
        update = jnp.dot(
            lax.all_gather(flat_tiles, "col", axis=1, tiled=True),
            whole_solved,
            preferred_element_type=jnp.float32,
        )
        remaining_rows = remaining_rows[1:] - update.reshape(later_count, tile_rows, rhs_width)
    return (jnp.stack(solved_list), remaining_rows)


def solution(mesh):
    in_specs = (P(None, "row", "col"), P(None, "row", None, "col"), P(None, "row", None))
    out_specs = (P(None, "row", "col"), P(None, "row", "col"))
    return jax.shard_map(shards, mesh=mesh, in_specs=in_specs, out_specs=out_specs, check_vma=False)
```

profile of v0, /device:TPU:0, one launch (start us, length us, event | category | flops | bytes accessed | tf_op | source)
XLA Modules:
  0.0 999.3 jit_solution(11575915859656223268)
XLA Ops:
  7.2 1.8 slice.102
  9.1 32.0 %all-gather.33.cloned.1.call-done = bf16[1,1024,1024]{2,1,0:T(8,128)(2,1)} async-done(((bf16[1,128,1024]{2,1,0:T(8,128)(2,1)}), bf16[1,1024,1024]{2,1,0:T(8,128)(2,1)}) %all-gather.33.cloned.1.call-update) | async-done | bytes 2097168 | tf_op jit(solution)/shard_map/all_gather | solution.py:19
  41.1 2.8 fusion.16
  44.0 8.8 slice.55
  52.8 3.9 copy.26
  56.8 0.0 all-gather.35.cloned.1.call-start
  56.8 15.2 %all-gather.17.cloned.1.call-done = bf16[1024,1024]{1,0:T(8,128)(2,1)} async-done(((bf16[128,1024]{1,0:T(8,128)(2,1)}), bf16[1024,1024]{1,0:T(8,128)(2,1)}) %all-gather.17.cloned.1.call-update) | async-done | bytes 2097168 | tf_op jit(solution)/shard_map/all_gather | solution.py:22
  72.0 147.0 %all-gather.19.cloned.1.call-done = bf16[3968,1024]{1,0:T(8,128)(2,1)} async-done(((bf16[3968,256]{1,0:T(8,128)(2,1)}), bf16[3968,1024]{1,0:T(8,128)(2,1)}) %all-gather.19.cloned.1.call-update) | async-done | bytes 8126480 | tf_op jit(solution)/shard_map/all_gather | solution.py:28
  219.0 15.9 %convolution_bitcast_fusion.3 = f32[3968,1024]{0,1:T(8,128)} fusion(bf16[1024,1024]{1,0:T(8,128)(2,1)} %all-gather.17.cloned.1.call-done, bf16[3968,1024]{1,0:T(8,128)(2,1)} %all-gather.19.cloned.1.call-done), kind=kOutput, calls=%fused_computation.7 | convolution fusion | flops 8321499136 | bytes 26476544 | tf_op jit(solution)/shard_map/dot_general | solution.py:27
  234.9 16.7 %copy.13 = f32[3968,1024]{1,0:T(8,128)} copy(f32[3968,1024]{0,1:T(8,128)} %convolution_bitcast_fusion.3) | data formatting | bytes 32505856 | tf_op jit(solution)/shard_map/dot_general | solution.py:27
  251.7 11.5 %slice_subtract_fusion = f32[31,128,1024]{2,1,0:T(8,128)S(1)} fusion(f32[31,128,1024]{2,1,0:T(8,128)} %bitcast.77, f32[32,128,1024]{2,1,0:T(8,128)} %param.3), kind=kLoop, calls=%fused_computation | loop fusion | flops 4063232 | bytes 48758784 | tf_op jit(solution)/shard_map/sub | solution.py:32
  263.2 5.6 copy-done
  268.8 0.7 slice.101
  269.5 0.5 all-gather.23.cloned.1.call-start
  270.0 10.0 %slice.59 = bf16[30,128,1,256]{3,2,1,0:T(2,128)(2,1)} slice(bf16[32,128,4,256]{3,2,1,0:T(4,128)(2,1)} %param.4), slice={[2:32], [0:128], [1:2], [0:256]} | slice | bytes 3932160 | tf_op jit(solution)/shard_map/slice | solution.py:25
  280.0 3.9 copy.27
  284.0 11.8 %all-gather.35.cloned.1.call-done = bf16[1,1024,1024]{2,1,0:T(8,128)(2,1)} async-done(((bf16[1,128,1024]{2,1,0:T(8,128)(2,1)}), bf16[1,1024,1024]{2,1,0:T(8,128)(2,1)}) %all-gather.35.cloned.1.call-update) | async-done | bytes 2097168 | tf_op jit(solution)/shard_map/all_gather | solution.py:19
  295.7 2.7 bitcast_convert_fusion.2
  298.6 139.8 %all-gather.23.cloned.1.call-done = bf16[3840,1024]{1,0:T(8,128)(2,1)} async-done(((bf16[3840,256]{1,0:T(8,128)(2,1)}), bf16[3840,1024]{1,0:T(8,128)(2,1)}) %all-gather.23.cloned.1.call-update) | async-done | bytes 7864336 | tf_op jit(solution)/shard_map/all_gather | solution.py:28
  438.3 28.4 %all-gather.21.cloned.1.call-done = bf16[1024,1024]{1,0:T(8,128)(2,1)} async-done(((bf16[128,1024]{1,0:T(8,128)(2,1)}), bf16[1024,1024]{1,0:T(8,128)(2,1)}) %all-gather.21.cloned.1.call-update) | async-done | bytes 2097168 | tf_op jit(solution)/shard_map/all_gather | solution.py:22
  466.8 15.3 %convolution_bitcast_fusion.2 = f32[3840,1024]{0,1:T(8,128)} fusion(bf16[1024,1024]{1,0:T(8,128)(2,1)} %all-gather.21.cloned.1.call-done, bf16[3840,1024]{1,0:T(8,128)(2,1)} %all-gather.23.cloned.1.call-done), kind=kOutput, calls=%fused_computation.6 | convolution fusion | flops 8053063680 | bytes 25690112 | tf_op jit(solution)/shard_map/dot_general | solution.py:27
  482.1 15.7 %copy.16 = f32[3840,1024]{1,0:T(8,128)} copy(f32[3840,1024]{0,1:T(8,128)} %convolution_bitcast_fusion.2) | data formatting | bytes 31457280 | tf_op jit(solution)/shard_map/dot_general | solution.py:27
  497.8 11.2 %slice_subtract_fusion.1 = f32[30,128,1024]{2,1,0:T(8,128)S(1)} fusion(f32[30,128,1024]{2,1,0:T(8,128)} %bitcast.78, f32[31,128,1024]{2,1,0:T(8,128)} %copy-done), kind=kLoop, calls=%fused_computation.1 | loop fusion | flops 3932160 | bytes 47185920 | tf_op jit(solution)/shard_map/sub | solution.py:32
  508.9 5.4 copy-done.1
  514.3 0.7 slice.100
  515.1 0.2 all-gather.27.cloned.1.call-start
  515.3 9.6 slice.63
  524.9 3.8 copy.28
  528.8 14.4 %all-gather.37.cloned.1.call-done = bf16[1,1024,1024]{2,1,0:T(8,128)(2,1)} async-done(((bf16[1,128,1024]{2,1,0:T(8,128)(2,1)}), bf16[1,1024,1024]{2,1,0:T(8,128)(2,1)}) %all-gather.37.cloned.1.call-update) | async-done | bytes 2097168 | tf_op jit(solution)/shard_map/all_gather | solution.py:19
  543.2 2.9 bitcast_convert_fusion.1
  546.1 135.5 %all-gather.27.cloned.1.call-done = bf16[3712,1024]{1,0:T(8,128)(2,1)} async-done(((bf16[3712,256]{1,0:T(8,128)(2,1)}), bf16[3712,1024]{1,0:T(8,128)(2,1)}) %all-gather.27.cloned.1.call-update) | async-done | bytes 7602192 | tf_op jit(solution)/shard_map/all_gather | solution.py:28
  681.6 28.6 %all-gather.25.cloned.1.call-done = bf16[1024,1024]{1,0:T(8,128)(2,1)} async-done(((bf16[128,1024]{1,0:T(8,128)(2,1)}), bf16[1024,1024]{1,0:T(8,128)(2,1)}) %all-gather.25.cloned.1.call-update) | async-done | bytes 2097168 | tf_op jit(solution)/shard_map/all_gather | solution.py:22
  710.2 15.1 %convolution_bitcast_fusion.1 = f32[3712,1024]{0,1:T(8,128)} fusion(bf16[1024,1024]{1,0:T(8,128)(2,1)} %all-gather.25.cloned.1.call-done, bf16[3712,1024]{1,0:T(8,128)(2,1)} %all-gather.27.cloned.1.call-done), kind=kOutput, calls=%fused_computation.5 | convolution fusion | flops 7784628224 | bytes 24903680 | tf_op jit(solution)/shard_map/dot_general | solution.py:27
  725.3 15.5 %copy.19 = f32[3712,1024]{1,0:T(8,128)} copy(f32[3712,1024]{0,1:T(8,128)} %convolution_bitcast_fusion.1) | data formatting | bytes 30408704 | tf_op jit(solution)/shard_map/dot_general | solution.py:27
  740.8 10.8 %slice_subtract_fusion.2 = f32[29,128,1024]{2,1,0:T(8,128)S(1)} fusion(f32[29,128,1024]{2,1,0:T(8,128)} %bitcast.79, f32[30,128,1024]{2,1,0:T(8,128)} %copy-done.1), kind=kLoop, calls=%fused_computation.2 | loop fusion | flops 3801088 | bytes 45613056 | tf_op jit(solution)/shard_map/sub | solution.py:32
  751.7 5.3 copy-done.2
  757.0 0.7 slice.99
  757.7 0.3 all-gather.31.cloned.1.call-start
  758.0 7.5 slice.67
  765.5 1.7 copy.29
  767.2 18.6 %all-gather.39.cloned.1.call-done = bf16[1,1024,1024]{2,1,0:T(8,128)(2,1)} async-done(((bf16[1,128,1024]{2,1,0:T(8,128)(2,1)}), bf16[1,1024,1024]{2,1,0:T(8,128)(2,1)}) %all-gather.39.cloned.1.call-update) | async-done | bytes 2097168 | tf_op jit(solution)/shard_map/all_gather | solution.py:19
  785.8 2.9 bitcast_convert_fusion
  788.7 2.6 pad_maximum_fusion
  791.3 128.7 %all-gather.31.cloned.1.call-done = bf16[3584,1024]{1,0:T(8,128)(2,1)} async-done(((bf16[3584,256]{1,0:T(8,128)(2,1)}), bf16[3584,1024]{1,0:T(8,128)(2,1)}) %all-gather.31.cloned.1.call-update) | async-done | bytes 7340048 | tf_op jit(solution)/shard_map/all_gather | solution.py:28
  920.0 27.9 %all-gather.29.cloned.1.call-done = bf16[1024,1024]{1,0:T(8,128)(2,1)} async-done(((bf16[128,1024]{1,0:T(8,128)(2,1)}), bf16[1024,1024]{1,0:T(8,128)(2,1)}) %all-gather.29.cloned.1.call-update) | async-done | bytes 2097168 | tf_op jit(solution)/shard_map/all_gather | solution.py:22
  947.8 13.8 %convolution_bitcast_fusion = f32[3584,1024]{0,1:T(8,128)} fusion(bf16[1024,1024]{1,0:T(8,128)(2,1)} %all-gather.29.cloned.1.call-done, bf16[3584,1024]{1,0:T(8,128)(2,1)} %all-gather.31.cloned.1.call-done), kind=kOutput, calls=%fused_computation.4 | convolution fusion | flops 7516192768 | bytes 24117248 | tf_op jit(solution)/shard_map/dot_general | solution.py:27
  961.6 15.4 %copy.22 = f32[3584,1024]{1,0:T(8,128)} copy(f32[3584,1024]{0,1:T(8,128)} %convolution_bitcast_fusion) | data formatting | bytes 29360128 | tf_op jit(solution)/shard_map/dot_general | solution.py:27
  977.0 15.2 %slice_subtract_fusion.3 = f32[28,128,1024]{2,1,0:T(8,128)} fusion(f32[28,128,1024]{2,1,0:T(8,128)} %bitcast.80, f32[29,128,1024]{2,1,0:T(8,128)} %copy-done.2), kind=kLoop, calls=%fused_computation.3 | loop fusion | flops 3670016 | bytes 44040192 | tf_op jit(solution)/shard_map/sub | solution.py:32
  (25 shorter events, 0.5 us)
Async XLA Ops:
  7.2 33.9 %all-gather.33.cloned.1.call-start = ((), (), s32[]{:S(2)}) async-start(), calls=%async_computation.8 | async-start | bytes 2359296 | tf_op jit(solution)/shard_map/all_gather | solution.py:19
  9.0 63.0 %all-gather.17.cloned.1.call-start = ((), (), s32[]{:S(2)}) async-start(), calls=%async_computation | async-start | bytes 2359296 | tf_op jit(solution)/shard_map/all_gather | solution.py:22
  44.0 175.1 %all-gather.19.cloned.1.call-start = ((), (), s32[]{:S(2)}) async-start(), calls=%async_computation.1 | async-start | bytes 10158080 | tf_op jit(solution)/shard_map/all_gather | solution.py:28
  56.8 239.0 %all-gather.35.cloned.1.call-start = ((), (), s32[]{:S(2)}) async-start(), calls=%async_computation.9 | async-start | bytes 2359296 | tf_op jit(solution)/shard_map/all_gather | solution.py:19
  263.2 5.6 copy-start
  269.5 26.2 %copy-start.3 = (bf16[4,128,1024]{2,1,0:T(8,128)(2,1)S(1)}, bf16[4,128,1024]{2,1,0:T(8,128)(2,1)}, u32[]{:S(2)}) copy-start(bf16[4,128,1024]{2,1,0:T(8,128)(2,1)} %param.5) | copy-start | bytes 3145732
  269.5 168.8 %all-gather.23.cloned.1.call-start = ((), (), s32[]{:S(2)}) async-start(), calls=%async_computation.3 | async-start | bytes 9830400 | tf_op jit(solution)/shard_map/all_gather | solution.py:28
  283.9 182.8 %all-gather.21.cloned.1.call-start = ((), (), s32[]{:S(2)}) async-start(), calls=%async_computation.2 | async-start | bytes 2359296 | tf_op jit(solution)/shard_map/all_gather | solution.py:22
  298.5 244.6 %all-gather.37.cloned.1.call-start = ((), (), s32[]{:S(2)}) async-start(), calls=%async_computation.10 | async-start | bytes 2359296 | tf_op jit(solution)/shard_map/all_gather | solution.py:19
  508.9 5.4 copy-start.1
  515.1 166.5 %all-gather.27.cloned.1.call-start = ((), (), s32[]{:S(2)}) async-start(), calls=%async_computation.5 | async-start | bytes 9502720 | tf_op jit(solution)/shard_map/all_gather | solution.py:28
  528.7 181.5 %all-gather.25.cloned.1.call-start = ((), (), s32[]{:S(2)}) async-start(), calls=%async_computation.4 | async-start | bytes 2359296 | tf_op jit(solution)/shard_map/all_gather | solution.py:22
  546.1 239.7 %all-gather.39.cloned.1.call-start = ((), (), s32[]{:S(2)}) async-start(), calls=%async_computation.11 | async-start | bytes 2359296 | tf_op jit(solution)/shard_map/all_gather | solution.py:19
  751.6 5.3 copy-start.2
  757.7 162.2 %all-gather.31.cloned.1.call-start = ((), (), s32[]{:S(2)}) async-start(), calls=%async_computation.7 | async-start | bytes 9175040 | tf_op jit(solution)/shard_map/all_gather | solution.py:28
  767.2 180.6 %all-gather.29.cloned.1.call-start = ((), (), s32[]{:S(2)}) async-start(), calls=%async_computation.6 | async-start | bytes 2359296 | tf_op jit(solution)/shard_map/all_gather | solution.py:22
Sparse Core Ops, SparseCore 0:
  10.5 30.5 all-gather.32
  44.1 27.8 all-gather.16
  74.1 144.8 all-gather.18
  269.6 26.0 all-gather.34
  297.7 140.5 all-gather.22
  440.6 26.0 all-gather.20
  515.2 27.8 all-gather.36
  545.3 136.2 all-gather.26
  684.1 26.0 all-gather.24
  757.9 27.8 all-gather.38
  787.9 131.9 all-gather.30
  921.7 26.0 all-gather.28
where the time goes:
time: 1010 us; the launch traced here: 999 us
  waiting for transfers between devices  728 us (72%)
  local copies, waits for them, and re-layouts  133 us (13%)
  matrix products  71.6 us (7%)
  other arithmetic  51.3 us (5%)
  between operations  14.5 us (1%)
    all_gather x4, waiting for transfers between devices, shards(): lax.all_gather(flat_tiles, 'col', axis=1, tiled=True)  551 us
    all_gather x4, waiting for transfers between devices, shards(): lax.all_gather(own_rows.astype(jnp.bfloat16), 'row', axis=0, tiled=True)  100 us
    all_gather x4, waiting for transfers between devices, shards(): lax.all_gather(current, 'row', axis=0, tiled=True)  76.7 us
    dot_general x4, local copies, waits for them, and re-layouts, shards(): jnp.dot(lax.all_gather(flat_tiles, 'col', axis=1, tiled=True), whole_solv...  63.3 us
    dot_general x4, matrix products, shards(): jnp.dot(lax.all_gather(flat_tiles, 'col', axis=1, tiled=True), whole_solv...  60.2 us
    sub x4, other arithmetic, shards(): remaining_rows[1:] - update.reshape(later_count, tile_rows, rhs_width)  48.7 us
    slice x4, local copies, waits for them, and re-layouts, shards(): lower_tiles = factor[section + 1:, :, section, :]  35.8 us
    unnamed x12, local copies, waits for them, and re-layouts  29.6 us
  transfers between devices with their start and end apart: 12, of which 12 were waited for; matrix products, arithmetic and copies ran while one was open for 6% of the time, Pallas kernels for 0%

commit v1 on v0

--- a/solution.py
+++ b/solution.py
@@ -4,6 +4,27 @@
 from jax.sharding import PartitionSpec as P
 
 STEPS = 4
+
+
+def gather_around(shard, axis, dim):
+    count, index, rows = (lax.axis_size(axis), lax.axis_index(axis), shard.shape[dim])
+    right = [(i, (i + 1) % count) for i in range(count)]
+    left = [(i, (i - 1) % count) for i in range(count)]
+    whole = jnp.zeros((*shard.shape[:dim], count * rows, *shard.shape[dim + 1 :]), shard.dtype)
+    whole = lax.dynamic_update_slice_in_dim(whole, shard, index * rows, axis=dim)
+    from_left = from_right = shard
+    half = count // 2
+    for lap in range(1, half + 1):
+        from_left = lax.ppermute(from_left, axis, right)
+        whole = lax.dynamic_update_slice_in_dim(
+            whole, from_left, (index - lap) % count * rows, axis=dim
+        )
+        if lap < count - half:
+            from_right = lax.ppermute(from_right, axis, left)
+            whole = lax.dynamic_update_slice_in_dim(
+                whole, from_right, (index + lap) % count * rows, axis=dim
+            )
+    return whole
 
 
 def shards(rhs, factor, diag_inverse):
@@ -15,9 +36,7 @@
         current = remaining_rows[0].astype(jnp.bfloat16)
         inverse_section = diag_inverse[section]
         own_rows = jnp.dot(
-            inverse_section,
-            lax.all_gather(current, "row", axis=0, tiled=True),
-            preferred_element_type=jnp.float32,
+            inverse_section, gather_around(current, "row", 0), preferred_element_type=jnp.float32
         )
         whole_solved = lax.all_gather(own_rows.astype(jnp.bfloat16), "row", axis=0, tiled=True)
         solved_list.append(own_rows)

time: 1010 us -> 779 us (0.77)
  waiting for transfers between devices: 728 us -> 468 us
  starting transfers between devices: 1.35 us -> 35.8 us
    all_gather x4, waiting for transfers between devices: 551 us -> 284 us  [shards(): lax.all_gather(flat_tiles, 'col', axis=1, tiled=True)]
    ppermute x0 -> x28, waiting for transfers between devices: none -> 92.2 us  [the longest x16 88 us: gather_around(): from_left = lax.ppermute(from_left, axis, right)]
    all_gather x4 -> x0, waiting for transfers between devices: 76.7 us -> none  [shards(): lax.all_gather(current, 'row', axis=0, tiled=True)]
    ppermute x0 -> x28, starting transfers between devices: none -> 34.6 us  [the longest x12 32.4 us: gather_around(): from_right = lax.ppermute(from_right, axis, left)]
    unnamed x12 -> x13, local copies, waits for them, and re-layouts: 29.6 us -> 30.5 us
  transfers between devices with their start and end apart: 12 -> 36, of which waited for: 12 -> 27; matrix products, arithmetic and copies ran while one was open for 6% -> 24% of each run, Pallas kernels for 0% -> 0%
where the time goes in v1:
time: 779 us; the launch traced here: 770 us
  waiting for transfers between devices  468 us (60%)
  local copies, waits for them, and re-layouts  133 us (17%)
  matrix products  68.1 us (9%)
  other arithmetic  50.6 us (6%)
  starting transfers between devices  35.8 us (5%)
  between operations  14.8 us (2%)
    all_gather x4, waiting for transfers between devices, shards(): lax.all_gather(flat_tiles, 'col', axis=1, tiled=True)  284 us
    all_gather x4, waiting for transfers between devices, shards(): lax.all_gather(own_rows.astype(jnp.bfloat16), 'row', axis=0, tiled=True)  92.1 us
    ppermute x16, waiting for transfers between devices, gather_around(): from_left = lax.ppermute(from_left, axis, right)  88 us
    dot_general x4, local copies, waits for them, and re-layouts, shards(): jnp.dot(lax.all_gather(flat_tiles, 'col', axis=1, tiled=True), whole_solv...  63.5 us
    dot_general x4, matrix products, shards(): jnp.dot(lax.all_gather(flat_tiles, 'col', axis=1, tiled=True), whole_solv...  60 us
    sub x4, other arithmetic, shards(): remaining_rows[1:] - update.reshape(later_count, tile_rows, rhs_width)  49.3 us
    slice x4, local copies, waits for them, and re-layouts, shards(): lower_tiles = factor[section + 1:, :, section, :]  36.2 us
    ppermute x12, starting transfers between devices, gather_around(): from_right = lax.ppermute(from_right, axis, left)  32.4 us
  transfers between devices with their start and end apart: 36, of which 27 were waited for; matrix products, arithmetic and copies ran while one was open for 24% of the time, Pallas kernels for 0%

profile of v1, /device:TPU:0, one launch (start us, length us, event | category | flops | bytes accessed | tf_op | source)
XLA Modules:
  0.0 770.3 jit_solution(4459046066774030571)
XLA Ops:
  9.1 2.9 collective-permute-start.1
  12.0 4.1 collective-permute-done
  17.7 2.8 collective-permute-start.3
  25.3 2.8 collective-permute-start.5
  32.0 5.2 collective-permute-done.6
  39.6 8.8 %slice.55 = bf16[31,128,1,256]{3,2,1,0:T(2,128)(2,1)} slice(bf16[32,128,4,256]{3,2,1,0:T(4,128)(2,1)} %param.4), slice={[1:32], [0:128], [0:1], [0:256]} | slice | bytes 4063232 | tf_op jit(solution)/shard_map/slice | solution.py:44
  48.4 3.9 copy.19
  52.4 10.2 %slice.59 = bf16[30,128,1,256]{3,2,1,0:T(2,128)(2,1)} slice(bf16[32,128,4,256]{3,2,1,0:T(4,128)(2,1)} %param.4), slice={[2:32], [0:128], [1:2], [0:256]} | slice | bytes 3932160 | tf_op jit(solution)/shard_map/slice | solution.py:44
  62.7 3.8 copy.20
  67.0 7.5 all-gather.9.cloned.1.call-done
  74.5 147.0 %all-gather.11.cloned.1.call-done = bf16[3968,1024]{1,0:T(8,128)(2,1)} async-done(((bf16[3968,256]{1,0:T(8,128)(2,1)}), bf16[3968,1024]{1,0:T(8,128)(2,1)}) %all-gather.11.cloned.1.call-update) | async-done | bytes 8126480 | tf_op jit(solution)/shard_map/all_gather | solution.py:47
  221.5 15.9 %convolution_bitcast_fusion.3 = f32[3968,1024]{0,1:T(8,128)} fusion(bf16[1024,1024]{0,1:T(8,128)(2,1)} %all-gather.9.cloned.1.call-done, bf16[3968,1024]{1,0:T(8,128)(2,1)} %all-gather.11.cloned.1.call-done), kind=kOutput, calls=%fused_computation.7 | convolution fusion | flops 8321499136 | bytes 26476544 | tf_op jit(solution)/shard_map/dot_general | solution.py:46
  237.4 16.8 %copy.11 = f32[3968,1024]{1,0:T(8,128)} copy(f32[3968,1024]{0,1:T(8,128)} %convolution_bitcast_fusion.3) | data formatting | bytes 32505856 | tf_op jit(solution)/shard_map/dot_general | solution.py:46
  254.2 11.8 %slice_subtract_fusion = f32[31,128,1024]{2,1,0:T(8,128)S(1)} fusion(f32[31,128,1024]{2,1,0:T(8,128)} %bitcast.76, f32[32,128,1024]{2,1,0:T(8,128)} %param.3), kind=kLoop, calls=%fused_computation | loop fusion | flops 4063232 | bytes 48758784 | tf_op jit(solution)/shard_map/sub | solution.py:51
  266.2 5.3 copy-done
  274.3 5.0 collective-permute-done.7
  279.3 3.1 collective-permute-start.10
  282.4 5.0 collective-permute-done.9
  290.2 5.8 collective-permute-done.11
  296.1 6.6 collective-permute-done.13
  304.3 9.6 %slice.63 = bf16[29,128,1,256]{3,2,1,0:T(2,128)(2,1)} slice(bf16[32,128,4,256]{3,2,1,0:T(4,128)(2,1)} %param.4), slice={[3:32], [0:128], [2:3], [0:256]} | slice | bytes 3801088 | tf_op jit(solution)/shard_map/slice | solution.py:44
  313.9 3.8 copy.21
  317.9 43.9 %all-gather.15.cloned.1.call-done = bf16[3840,1024]{1,0:T(8,128)(2,1)} async-done(((bf16[3840,256]{1,0:T(8,128)(2,1)}), bf16[3840,1024]{1,0:T(8,128)(2,1)}) %all-gather.15.cloned.1.call-update) | async-done | bytes 7864336 | tf_op jit(solution)/shard_map/all_gather | solution.py:47
  361.9 28.1 %all-gather.13.cloned.1.call-done = bf16[1024,1024]{0,1:T(8,128)(2,1)} async-done(((bf16[128,1024]{0,1:T(8,128)(2,1)}), bf16[1024,1024]{0,1:T(8,128)(2,1)}) %all-gather.13.cloned.1.call-update) | async-done | bytes 2097168 | tf_op jit(solution)/shard_map/all_gather | solution.py:41
  390.0 15.2 %convolution_bitcast_fusion.2 = f32[3840,1024]{0,1:T(8,128)} fusion(bf16[1024,1024]{0,1:T(8,128)(2,1)} %all-gather.13.cloned.1.call-done, bf16[3840,1024]{1,0:T(8,128)(2,1)} %all-gather.15.cloned.1.call-done), kind=kOutput, calls=%fused_computation.6 | convolution fusion | flops 8053063680 | bytes 25690112 | tf_op jit(solution)/shard_map/dot_general | solution.py:46
  405.3 15.7 %copy.13 = f32[3840,1024]{1,0:T(8,128)} copy(f32[3840,1024]{0,1:T(8,128)} %convolution_bitcast_fusion.2) | data formatting | bytes 31457280 | tf_op jit(solution)/shard_map/dot_general | solution.py:46
  421.0 11.3 %slice_subtract_fusion.1 = f32[30,128,1024]{2,1,0:T(8,128)S(1)} fusion(f32[30,128,1024]{2,1,0:T(8,128)} %bitcast.77, f32[31,128,1024]{2,1,0:T(8,128)} %copy-done), kind=kLoop, calls=%fused_computation.1 | loop fusion | flops 3932160 | bytes 47185920 | tf_op jit(solution)/shard_map/sub | solution.py:51
  432.6 5.1 copy-done.1
  440.5 6.0 collective-permute-done.14
  449.2 6.5 collective-permute-done.16
  458.5 6.5 collective-permute-done.18
  465.1 6.6 collective-permute-done.20
  473.5 7.5 slice.67
  483.0 45.3 %all-gather.19.cloned.1.call-done = bf16[3712,1024]{1,0:T(8,128)(2,1)} async-done(((bf16[3712,256]{1,0:T(8,128)(2,1)}), bf16[3712,1024]{1,0:T(8,128)(2,1)}) %all-gather.19.cloned.1.call-update) | async-done | bytes 7602192 | tf_op jit(solution)/shard_map/all_gather | solution.py:47
  528.3 28.1 %all-gather.17.cloned.1.call-done = bf16[1024,1024]{0,1:T(8,128)(2,1)} async-done(((bf16[128,1024]{0,1:T(8,128)(2,1)}), bf16[1024,1024]{0,1:T(8,128)(2,1)}) %all-gather.17.cloned.1.call-update) | async-done | bytes 2097168 | tf_op jit(solution)/shard_map/all_gather | solution.py:41
  556.5 15.1 %convolution_bitcast_fusion.1 = f32[3712,1024]{0,1:T(8,128)} fusion(bf16[1024,1024]{0,1:T(8,128)(2,1)} %all-gather.17.cloned.1.call-done, bf16[3712,1024]{1,0:T(8,128)(2,1)} %all-gather.19.cloned.1.call-done), kind=kOutput, calls=%fused_computation.5 | convolution fusion | flops 7784628224 | bytes 24903680 | tf_op jit(solution)/shard_map/dot_general | solution.py:46
  571.6 15.6 %copy.15 = f32[3712,1024]{1,0:T(8,128)} copy(f32[3712,1024]{0,1:T(8,128)} %convolution_bitcast_fusion.1) | data formatting | bytes 30408704 | tf_op jit(solution)/shard_map/dot_general | solution.py:46
  587.2 11.0 %slice_subtract_fusion.2 = f32[29,128,1024]{2,1,0:T(8,128)S(1)} fusion(f32[29,128,1024]{2,1,0:T(8,128)} %bitcast.78, f32[30,128,1024]{2,1,0:T(8,128)} %copy-done.1), kind=kLoop, calls=%fused_computation.2 | loop fusion | flops 3801088 | bytes 45613056 | tf_op jit(solution)/shard_map/sub | solution.py:51
  598.5 5.0 copy-done.2
  606.3 6.1 collective-permute-done.21
  615.0 6.5 collective-permute-done.23
  624.3 6.5 collective-permute-done.25
  631.0 6.6 collective-permute-done.27
  643.3 47.3 %all-gather.23.cloned.1.call-done = bf16[3584,1024]{1,0:T(8,128)(2,1)} async-done(((bf16[3584,256]{1,0:T(8,128)(2,1)}), bf16[3584,1024]{1,0:T(8,128)(2,1)}) %all-gather.23.cloned.1.call-update) | async-done | bytes 7340048 | tf_op jit(solution)/shard_map/all_gather | solution.py:47
  690.6 28.3 %all-gather.21.cloned.1.call-done = bf16[1024,1024]{0,1:T(8,128)(2,1)} async-done(((bf16[128,1024]{0,1:T(8,128)(2,1)}), bf16[1024,1024]{0,1:T(8,128)(2,1)}) %all-gather.21.cloned.1.call-update) | async-done | bytes 2097168 | tf_op jit(solution)/shard_map/all_gather | solution.py:41
  718.9 13.8 %convolution_bitcast_fusion = f32[3584,1024]{0,1:T(8,128)} fusion(bf16[1024,1024]{0,1:T(8,128)(2,1)} %all-gather.21.cloned.1.call-done, bf16[3584,1024]{1,0:T(8,128)(2,1)} %all-gather.23.cloned.1.call-done), kind=kOutput, calls=%fused_computation.4 | convolution fusion | flops 7516192768 | bytes 24117248 | tf_op jit(solution)/shard_map/dot_general | solution.py:46
  732.7 15.4 %copy.17 = f32[3584,1024]{1,0:T(8,128)} copy(f32[3584,1024]{0,1:T(8,128)} %convolution_bitcast_fusion) | data formatting | bytes 29360128 | tf_op jit(solution)/shard_map/dot_general | solution.py:46
  748.1 15.2 %slice_subtract_fusion.3 = f32[28,128,1024]{2,1,0:T(8,128)} fusion(f32[28,128,1024]{2,1,0:T(8,128)} %bitcast.79, f32[29,128,1024]{2,1,0:T(8,128)} %copy-done.2), kind=kLoop, calls=%fused_computation.3 | loop fusion | flops 3670016 | bytes 44040192 | tf_op jit(solution)/shard_map/sub | solution.py:51
  (102 shorter events, 49.2 us)
Async XLA Ops:
  7.2 67.4 %all-gather.9.cloned.1.call-start = ((), (), s32[]{:S(2)}) async-start(), calls=%async_computation | async-start | bytes 2359296 | tf_op jit(solution)/shard_map/all_gather | solution.py:41
  8.6 7.6 collective-permute-start
  9.1 8.6 %collective-permute-start.1 = (bf16[128,1024]{1,0:T(8,128)(2,1)S(1)}, bf16[128,1024]{1,0:T(8,128)(2,1)S(1)}, u32[]{:S(2)}, u32[]{:S(2)}) collective-permute-start(bf16[128,1024]{1,0:T(8,128)(2,1)S(1)} %get-tuple-element.13), channel_id=1, source_target_pairs={{0,28},{4,0},{8,4},{12,8},{16,12},{20,16},{24,20},{28,24},{1,29},{... | collective-permute-start | bytes 786440 | tf_op jit(solution)/shard_map/ppermute | solution.py:23
  16.2 6.9 collective-permute-start.2
  17.7 7.6 collective-permute-start.3
  23.0 7.4 collective-permute-start.4
  25.3 6.7 collective-permute-start.5
  30.5 6.7 collective-permute-start.6
  39.6 181.9 %all-gather.11.cloned.1.call-start = ((), (), s32[]{:S(2)}) async-start(), calls=%async_computation.1 | async-start | bytes 10158080 | tf_op jit(solution)/shard_map/all_gather | solution.py:47
  52.4 309.5 %all-gather.15.cloned.1.call-start = ((), (), s32[]{:S(2)}) async-start(), calls=%async_computation.3 | async-start | bytes 9830400 | tf_op jit(solution)/shard_map/all_gather | solution.py:47
  66.5 323.5 %all-gather.13.cloned.1.call-start = ((), (), s32[]{:S(2)}) async-start(), calls=%async_computation.2 | async-start | bytes 2359296 | tf_op jit(solution)/shard_map/all_gather | solution.py:41
  266.0 5.6 copy-start
  271.5 31.2 %copy-start.3 = (bf16[4,128,1024]{2,1,0:T(8,128)(2,1)S(1)}, bf16[4,128,1024]{2,1,0:T(8,128)(2,1)}, u32[]{:S(2)}) copy-start(bf16[4,128,1024]{2,1,0:T(8,128)(2,1)} %param.5) | copy-start | bytes 3145732
  271.6 7.7 %collective-permute-start.7 = (bf16[128,1024]{1,0:T(8,128)(2,1)S(1)}, bf16[128,1024]{1,0:T(8,128)(2,1)S(1)}, u32[]{:S(2)}, u32[]{:S(2)}) collective-permute-start(bf16[128,1024]{1,0:T(8,128)(2,1)S(1)} %get-tuple-element.11), channel_id=1, source_target_pairs={{0,4},{4,8},{8,12},{12,16},{16,20},{20,24},{24,28},{28,0},{1,5},{5... | collective-permute-start | bytes 786440 | tf_op jit(solution)/shard_map/ppermute | solution.py:18
  271.7 7.6 collective-permute-start.8
  279.3 8.1 %collective-permute-start.9 = (bf16[128,1024]{1,0:T(8,128)(2,1)S(1)}, bf16[128,1024]{1,0:T(8,128)(2,1)S(1)}, u32[]{:S(2)}, u32[]{:S(2)}) collective-permute-start(bf16[128,1024]{1,0:T(8,128)(2,1)S(1)} %collective-permute-done.7), channel_id=1, source_target_pairs={{0,4},{4,8},{8,12},{12,16},{16,20},{20,24},{24,28},{28,0},{1,5},{5... | collective-permute-start | bytes 786440 | tf_op jit(solution)/shard_map/ppermute | solution.py:18
  279.3 8.2 %collective-permute-start.10 = (bf16[128,1024]{1,0:T(8,128)(2,1)S(1)}, bf16[128,1024]{1,0:T(8,128)(2,1)S(1)}, u32[]{:S(2)}, u32[]{:S(2)}) collective-permute-start(bf16[128,1024]{1,0:T(8,128)(2,1)S(1)} %collective-permute-done.8), channel_id=1, source_target_pairs={{0,28},{4,0},{8,4},{12,8},{16,12},{20,16},{24,20},{28,24},{1,29},{... | collective-permute-start | bytes 786440 | tf_op jit(solution)/shard_map/ppermute | solution.py:23
  287.4 8.6 %collective-permute-start.11 = (bf16[128,1024]{1,0:T(8,128)(2,1)S(1)}, bf16[128,1024]{1,0:T(8,128)(2,1)S(1)}, u32[]{:S(2)}, u32[]{:S(2)}) collective-permute-start(bf16[128,1024]{1,0:T(8,128)(2,1)S(1)} %collective-permute-done.9), channel_id=1, source_target_pairs={{0,4},{4,8},{8,12},{12,16},{16,20},{20,24},{24,28},{28,0},{1,5},{5... | collective-permute-start | bytes 786440 | tf_op jit(solution)/shard_map/ppermute | solution.py:18
  287.5 8.6 %collective-permute-start.12 = (bf16[128,1024]{1,0:T(8,128)(2,1)S(1)}, bf16[128,1024]{1,0:T(8,128)(2,1)S(1)}, u32[]{:S(2)}, u32[]{:S(2)}) collective-permute-start(bf16[128,1024]{1,0:T(8,128)(2,1)S(1)} %collective-permute-done.10), channel_id=1, source_target_pairs={{0,28},{4,0},{8,4},{12,8},{16,12},{20,16},{24,20},{28,24},{1,29},{... | collective-permute-start | bytes 786440 | tf_op jit(solution)/shard_map/ppermute | solution.py:23
  296.0 6.7 collective-permute-start.13
  304.2 224.1 %all-gather.19.cloned.1.call-start = ((), (), s32[]{:S(2)}) async-start(), calls=%async_computation.5 | async-start | bytes 9502720 | tf_op jit(solution)/shard_map/all_gather | solution.py:47
  317.7 238.8 %all-gather.17.cloned.1.call-start = ((), (), s32[]{:S(2)}) async-start(), calls=%async_computation.4 | async-start | bytes 2359296 | tf_op jit(solution)/shard_map/all_gather | solution.py:41
  432.3 5.4 copy-start.1
  437.8 8.7 %collective-permute-start.14 = (bf16[128,1024]{1,0:T(8,128)(2,1)S(1)}, bf16[128,1024]{1,0:T(8,128)(2,1)S(1)}, u32[]{:S(2)}, u32[]{:S(2)}) collective-permute-start(bf16[128,1024]{1,0:T(8,128)(2,1)S(1)} %get-tuple-element.9), channel_id=1, source_target_pairs={{0,4},{4,8},{8,12},{12,16},{16,20},{20,24},{24,28},{28,0},{1,5},{5... | collective-permute-start | bytes 786440 | tf_op jit(solution)/shard_map/ppermute | solution.py:18
  438.1 8.4 %collective-permute-start.15 = (bf16[128,1024]{1,0:T(8,128)(2,1)S(1)}, bf16[128,1024]{1,0:T(8,128)(2,1)S(1)}, u32[]{:S(2)}, u32[]{:S(2)}) collective-permute-start(bf16[128,1024]{1,0:T(8,128)(2,1)S(1)} %get-tuple-element.9), channel_id=1, source_target_pairs={{0,28},{4,0},{8,4},{12,8},{16,12},{20,16},{24,20},{28,24},{1,29},{... | collective-permute-start | bytes 786440 | tf_op jit(solution)/shard_map/ppermute | solution.py:23
  446.5 9.2 %collective-permute-start.16 = (bf16[128,1024]{1,0:T(8,128)(2,1)S(1)}, bf16[128,1024]{1,0:T(8,128)(2,1)S(1)}, u32[]{:S(2)}, u32[]{:S(2)}) collective-permute-start(bf16[128,1024]{1,0:T(8,128)(2,1)S(1)} %collective-permute-done.14), channel_id=1, source_target_pairs={{0,4},{4,8},{8,12},{12,16},{16,20},{20,24},{24,28},{28,0},{1,5},{5... | collective-permute-start | bytes 786440 | tf_op jit(solution)/shard_map/ppermute | solution.py:18
  446.5 9.2 %collective-permute-start.17 = (bf16[128,1024]{1,0:T(8,128)(2,1)S(1)}, bf16[128,1024]{1,0:T(8,128)(2,1)S(1)}, u32[]{:S(2)}, u32[]{:S(2)}) collective-permute-start(bf16[128,1024]{1,0:T(8,128)(2,1)S(1)} %collective-permute-done.15), channel_id=1, source_target_pairs={{0,28},{4,0},{8,4},{12,8},{16,12},{20,16},{24,20},{28,24},{1,29},{... | collective-permute-start | bytes 786440 | tf_op jit(solution)/shard_map/ppermute | solution.py:23
  455.7 9.3 %collective-permute-start.18 = (bf16[128,1024]{1,0:T(8,128)(2,1)S(1)}, bf16[128,1024]{1,0:T(8,128)(2,1)S(1)}, u32[]{:S(2)}, u32[]{:S(2)}) collective-permute-start(bf16[128,1024]{1,0:T(8,128)(2,1)S(1)} %collective-permute-done.16), channel_id=1, source_target_pairs={{0,4},{4,8},{8,12},{12,16},{16,20},{20,24},{24,28},{28,0},{1,5},{5... | collective-permute-start | bytes 786440 | tf_op jit(solution)/shard_map/ppermute | solution.py:18
  455.8 9.3 %collective-permute-start.19 = (bf16[128,1024]{1,0:T(8,128)(2,1)S(1)}, bf16[128,1024]{1,0:T(8,128)(2,1)S(1)}, u32[]{:S(2)}, u32[]{:S(2)}) collective-permute-start(bf16[128,1024]{1,0:T(8,128)(2,1)S(1)} %collective-permute-done.17), channel_id=1, source_target_pairs={{0,28},{4,0},{8,4},{12,8},{16,12},{20,16},{24,20},{28,24},{1,29},{... | collective-permute-start | bytes 786440 | tf_op jit(solution)/shard_map/ppermute | solution.py:23
  465.0 6.7 collective-permute-start.20
  473.5 217.2 %all-gather.23.cloned.1.call-start = ((), (), s32[]{:S(2)}) async-start(), calls=%async_computation.7 | async-start | bytes 9175040 | tf_op jit(solution)/shard_map/all_gather | solution.py:47
  482.8 236.2 %all-gather.21.cloned.1.call-start = ((), (), s32[]{:S(2)}) async-start(), calls=%async_computation.6 | async-start | bytes 2359296 | tf_op jit(solution)/shard_map/all_gather | solution.py:41
  598.2 5.3 copy-start.2
  603.6 8.8 %collective-permute-start.21 = (bf16[128,1024]{1,0:T(8,128)(2,1)S(1)}, bf16[128,1024]{1,0:T(8,128)(2,1)S(1)}, u32[]{:S(2)}, u32[]{:S(2)}) collective-permute-start(bf16[128,1024]{1,0:T(8,128)(2,1)S(1)} %get-tuple-element.7), channel_id=1, source_target_pairs={{0,4},{4,8},{8,12},{12,16},{16,20},{20,24},{24,28},{28,0},{1,5},{5... | collective-permute-start | bytes 786440 | tf_op jit(solution)/shard_map/ppermute | solution.py:18
  603.9 8.4 %collective-permute-start.22 = (bf16[128,1024]{1,0:T(8,128)(2,1)S(1)}, bf16[128,1024]{1,0:T(8,128)(2,1)S(1)}, u32[]{:S(2)}, u32[]{:S(2)}) collective-permute-start(bf16[128,1024]{1,0:T(8,128)(2,1)S(1)} %get-tuple-element.7), channel_id=1, source_target_pairs={{0,28},{4,0},{8,4},{12,8},{16,12},{20,16},{24,20},{28,24},{1,29},{... | collective-permute-start | bytes 786440 | tf_op jit(solution)/shard_map/ppermute | solution.py:23
  612.3 9.2 %collective-permute-start.23 = (bf16[128,1024]{1,0:T(8,128)(2,1)S(1)}, bf16[128,1024]{1,0:T(8,128)(2,1)S(1)}, u32[]{:S(2)}, u32[]{:S(2)}) collective-permute-start(bf16[128,1024]{1,0:T(8,128)(2,1)S(1)} %collective-permute-done.21), channel_id=1, source_target_pairs={{0,4},{4,8},{8,12},{12,16},{16,20},{20,24},{24,28},{28,0},{1,5},{5... | collective-permute-start | bytes 786440 | tf_op jit(solution)/shard_map/ppermute | solution.py:18
  612.3 9.3 %collective-permute-start.24 = (bf16[128,1024]{1,0:T(8,128)(2,1)S(1)}, bf16[128,1024]{1,0:T(8,128)(2,1)S(1)}, u32[]{:S(2)}, u32[]{:S(2)}) collective-permute-start(bf16[128,1024]{1,0:T(8,128)(2,1)S(1)} %collective-permute-done.22), channel_id=1, source_target_pairs={{0,28},{4,0},{8,4},{12,8},{16,12},{20,16},{24,20},{28,24},{1,29},{... | collective-permute-start | bytes 786440 | tf_op jit(solution)/shard_map/ppermute | solution.py:23
  621.5 9.3 %collective-permute-start.25 = (bf16[128,1024]{1,0:T(8,128)(2,1)S(1)}, bf16[128,1024]{1,0:T(8,128)(2,1)S(1)}, u32[]{:S(2)}, u32[]{:S(2)}) collective-permute-start(bf16[128,1024]{1,0:T(8,128)(2,1)S(1)} %collective-permute-done.23), channel_id=1, source_target_pairs={{0,4},{4,8},{8,12},{12,16},{16,20},{20,24},{24,28},{28,0},{1,5},{5... | collective-permute-start | bytes 786440 | tf_op jit(solution)/shard_map/ppermute | solution.py:18
  621.6 9.3 %collective-permute-start.26 = (bf16[128,1024]{1,0:T(8,128)(2,1)S(1)}, bf16[128,1024]{1,0:T(8,128)(2,1)S(1)}, u32[]{:S(2)}, u32[]{:S(2)}) collective-permute-start(bf16[128,1024]{1,0:T(8,128)(2,1)S(1)} %collective-permute-done.24), channel_id=1, source_target_pairs={{0,28},{4,0},{8,4},{12,8},{16,12},{20,16},{24,20},{28,24},{1,29},{... | collective-permute-start | bytes 786440 | tf_op jit(solution)/shard_map/ppermute | solution.py:23
  630.9 6.7 collective-permute-start.27
Sparse Core Ops, SparseCore 0:
  39.7 34.7 all-gather.8
  76.7 144.8 all-gather.10
  223.1 138.7 all-gather.14
  363.6 26.3 all-gather.12
  392.0 136.2 all-gather.18
  530.1 26.3 all-gather.16
  558.6 131.9 all-gather.22
  692.5 26.3 all-gather.20
